TPU v7x, 32 devices: a whole 2x2x4 slice. The times are simulated.
32 devices in a mesh: groups: 2 (over y), people: 4 (over z), blocks: 2 (over x), sub: 2 (over core).
Axes of the slice: x: 2, y: 2, z: 4, core: 2. Of those that a mesh axis runs over, the one named last changes fastest.
Arguments:
- dosage: int32 [4096, 2048], P(('groups', 'people', 'sub'), 'blocks'), parts along dimension 0, may hold values from 0 to 200
- fold: int32 [4096], P(('groups', 'people', 'sub')), parts along dimension 0, may hold values from 0 to 1, as said below
- pheno: bfloat16 [4096, 48], P(('groups', 'people', 'sub')), parts along dimension 0, may hold values from -8 to 8
- ridges: float32 [5], replicated, may hold values from 1 to 20
Outputs:
- second: float32 [48, 5, 4096], P(('blocks', 'sub'), None, ('groups', 'people')), parts along dimension 2
There are 2 independent parts, one for each index of `groups`. A program takes and returns all parts, laid end to end along the dimension named above; an argument that names none is the same for every part. Nothing has to cross between parts.
Inputs may be any that keep to these rules, and one draw needn't show every extreme that they name: Each fold holds exactly 1024 people.
All inputs are finite; a program needn't handle non-finite values.
Results may differ from a plain program's by a relative error of at most 0.0021.
Values may be sent and summed in bfloat16 or wider, within the bound.
No kernel may reach another device: no remote copies, remote signals or barrier semaphores. Data moves between devices by JAX's collectives and lax.ppermute only.
A program may use at most 64 MiB of HBM per device.

v0:
```python
import jax
import jax.numpy as jnp
from jax import lax
from jax.sharding import PartitionSpec as P

TRAITS = 48
RIDGES = 5
FOLDS = 2
ITERS = 10
ITERS_TWO = 4


highest = lax.Precision.HIGHEST


def conjugate(apply_system, right_side, steps):
    estimate = jnp.zeros_like(right_side)
    residual = right_side
    direction = right_side
    current = jnp.sum(residual * residual, -2, keepdims=True)
    for step in range(steps):
        image = apply_system(direction)
        alpha = current / jnp.sum(direction * image, -2, keepdims=True)
        estimate = estimate + alpha * direction
        residual = residual - alpha * image
        following = jnp.sum(residual * residual, -2, keepdims=True)
        direction = residual + following / current * direction
        current = following
    return estimate


def covariance_rows(gram_rows, row_sums, all_sums, row_mean, all_mean, train_count):
    return (
        gram_rows
        - row_sums[:, None] * all_mean[None, :]
        - row_mean[:, None] * all_sums[None, :]
        + train_count * row_mean[:, None] * all_mean[None, :]
    )


def train_total(pieces, fold_index):
    return sum([pieces[other] for other in range(FOLDS) if other != fold_index])


def system_rows(shares, sums_all, column_mean, column_spread, row_start, share_rows, train_count):
    row_mean = lax.dynamic_slice_in_dim(column_mean, row_start, share_rows, 0)
    row_spread = lax.dynamic_slice_in_dim(column_spread, row_start, share_rows, 0)
    systems = []
    for fold_index in range(FOLDS):
        sums_train = train_total(sums_all, fold_index)
        row_sums = lax.dynamic_slice_in_dim(sums_train, row_start, share_rows, 0)
        covariance = covariance_rows(
            train_total(shares, fold_index),
            row_sums,
            sums_train,
            row_mean,
            column_mean,
            train_count,
        )
        systems.append(covariance / (train_count * row_spread[:, None] * column_spread[None, :]))
    return (jnp.stack(systems), row_spread)


def shards(dosage, fold, pheno, ridges):
    row_count, block_size = dosage.shape
    people_count = lax.axis_size("people")
    sub_count = lax.axis_size("sub")
    people = row_count * people_count * sub_count
    train_count = people - people // FOLDS
    centred = (dosage - 100).astype(jnp.bfloat16)
    pheno_wide = pheno.astype(jnp.float32)
    masks = [fold[:, None] == fold_index for fold_index in range(FOLDS)]
    grams, sums, squares, cross, totals = ([], [], [], [], [])
    for mask in masks:
        masked = jnp.where(mask, centred, jnp.zeros_like(centred))
        grams.append(
            lax.dot_general(
                masked, centred, (((0,), (0,)), ((), ())), preferred_element_type=jnp.float32
            )
        )
        masked_wide = masked.astype(jnp.float32)
        sums.append(jnp.sum(masked_wide, 0))
        squares.append(jnp.sum(masked_wide * masked_wide, 0))
        cross.append(
            lax.dot_general(
                masked, pheno, (((0,), (0,)), ((), ())), preferred_element_type=jnp.float32
            )
        )
        totals.append(jnp.sum(jnp.where(mask, pheno_wide, 0.0), 0))
    sums_all, squares_all, cross_all, totals_all = lax.psum(
        (jnp.stack(sums), jnp.stack(squares), jnp.stack(cross), jnp.stack(totals)),
        ("people", "sub"),
    )
    column_mean = sum([sums_all[fold_index] for fold_index in range(FOLDS)]) / people
    column_spread = jnp.sqrt(
        sum([squares_all[fold_index] for fold_index in range(FOLDS)]) / people
        - column_mean * column_mean
        + 1e-05
    )
    right_sides = []
    for fold_index in range(FOLDS):
        right_sides.append(
            (
                train_total(cross_all, fold_index)
                - column_mean[:, None] * train_total(totals_all, fold_index)[None, :]
            )
            / (train_count * column_spread[:, None])
        )
    gram_stack = jnp.stack(grams)
    share_rows = block_size // (people_count * sub_count)
    row_start = (lax.axis_index("people") * sub_count + lax.axis_index("sub")) * share_rows
    shares = lax.psum_scatter(gram_stack, ("people", "sub"), scatter_dimension=1, tiled=True)
    systems, row_spread = system_rows(
        shares, sums_all, column_mean, column_spread, row_start, share_rows, train_count
    )
    whole = lax.all_gather(systems, ("people", "sub"), axis=1, tiled=True)
    own_fold = lax.axis_index("sub")
    system = lax.dynamic_index_in_dim(whole, own_fold, 0, keepdims=False)
    trait_share = TRAITS // people_count
    trait_start = lax.axis_index("people") * trait_share
    right_own = lax.dynamic_index_in_dim(jnp.stack(right_sides), own_fold, 0, keepdims=False)
    right_cols = lax.dynamic_slice_in_dim(right_own, trait_start, trait_share, 1)
    shifts = jnp.repeat(ridges, trait_share)
    estimate = conjugate(
        lambda direction: jnp.dot(system, direction, precision=highest) + shifts * direction,
        jnp.tile(right_cols, (1, RIDGES)),
        ITERS,
    )
    scaled = (estimate / column_spread[:, None]).astype(jnp.bfloat16)
    scaled = scaled.reshape(block_size, RIDGES, trait_share)
    gathered = lax.all_gather(scaled[None], ("people", "sub"), axis=0, tiled=True)
    coefficients = gathered.reshape(people_count, sub_count, block_size, RIDGES, trait_share)
    coefficients = coefficients.transpose(1, 2, 3, 0, 4).reshape(FOLDS, block_size, RIDGES * TRAITS)
    prediction = jnp.zeros((row_count, RIDGES * TRAITS), jnp.float32)
    for fold_index in range(FOLDS):
        offset = jnp.dot(
            column_mean, coefficients[fold_index].astype(jnp.float32), precision=highest
        )
        outcome = (
            jnp.dot(centred, coefficients[fold_index], preferred_element_type=jnp.float32) - offset
        )
        prediction = prediction + jnp.where(masks[fold_index], outcome, 0.0)
    prediction = prediction.astype(jnp.bfloat16).reshape(1, row_count, RIDGES, TRAITS)
    moved, moved_pheno = (
        lax.all_to_all(prediction, ("blocks", "sub"), split_axis=3, concat_axis=0, tiled=True),
        lax.all_to_all(
            pheno[None, :, None, :], ("blocks", "sub"), split_axis=3, concat_axis=0, tiled=True
        ),
    )
    block_count = lax.axis_size("blocks")
    trait_group = TRAITS // (block_count * sub_count)
    predictors = moved.reshape(block_count, sub_count, row_count, RIDGES, trait_group)
    predictors = predictors.transpose(1, 2, 4, 0, 3).reshape(
        sub_count * row_count, trait_group, block_count * RIDGES
    )
    targets = moved_pheno.reshape(block_count, sub_count, row_count, trait_group)[0]
    targets = targets.reshape(sub_count * row_count, trait_group)
    gram_two = jnp.einsum(
        "nta,ntb->tab", predictors, predictors, preferred_element_type=jnp.float32
    )
    cross_two = jnp.einsum("nt,nta->ta", targets, predictors, preferred_element_type=jnp.float32)
    gram_two, cross_two = lax.psum((gram_two, cross_two), "people")
    gram_two = gram_two / people
    cross_two = cross_two / people
    predictor_count = block_count * RIDGES
    level = jnp.trace(gram_two, axis1=1, axis2=2) / predictor_count + 1e-06
    level_shift = ridges[None, None, :] * level[:, None, None]
    right_two = jnp.broadcast_to(cross_two[:, :, None], (trait_group, predictor_count, RIDGES))
    weights = conjugate(
        lambda direction: jnp.einsum("tab,tbr->tar", gram_two, direction, precision=highest)
        + level_shift * direction,
        right_two,
        ITERS_TWO,
    )
    return jnp.einsum("nta,tar->trn", predictors.astype(jnp.float32), weights, precision=highest)


def solution(mesh):
    return jax.shard_map(
        shards,
        mesh=mesh,
        in_specs=(
            P(("groups", "people", "sub"), "blocks"),
            P(("groups", "people", "sub")),
            P(("groups", "people", "sub"), None),
            P(),
        ),
        out_specs=P(("blocks", "sub"), None, ("groups", "people")),
        check_vma=False,
    )
```

profile of v0, /device:TPU:0, one launch (start us, length us, event | category | flops | bytes accessed | tf_op | source)
XLA Modules:
  0.0 376.8 jit_solution(10997729040896676900)
XLA Ops:
  7.2 1.7 convert_reduce_fusion.1
  8.9 0.8 convolution_bitcast_fusion
  9.7 0.8 convolution_bitcast_fusion.1
  10.6 4.1 %pad_maximum_fusion = f32[2,1024,1024]{2,1,0:T(8,128)} fusion(f32[1,1024,1024]{2,1,0:T(8,128)S(1)} %convolution_bitcast_fusion, f32[1,1024,1024]{2,1,0:T(8,128)S(1)} %convolution_bitcast_fusion.1), kind=kLoop, calls=%fused_computation | loop fusion | flops 2097152 | bytes 16777216 | tf_op jit(solution)/shard_map/stack | solution.py:109
  15.9 0.8 pad_maximum_fusion.2
  17.0 31.7 %all-reduce = (f32[2,1024]{1,0:T(2,128)S(1)}, f32[2,1024]{1,0:T(2,128)S(1)}, f32[2,48]{1,0:T(2,128)S(1)}) all-reduce(f32[2,1024]{1,0:T(2,128)S(1)} %get-tuple-element.88, f32[2,1024]{1,0:T(2,128)S(1)} %get-tuple-element.87, f32[2,48]{1,0:T(2,128)S(1)} %pad_maximum_fusion.5), channel_id=1, replica_groups=mesh['groups'=2,'people'=4,'blocks'=2,'sub'=2] {'people','sub'}, use_global_device_ids=true, to_apply=%region_9.10 | all-reduce | flops 4192 | bytes 33536 | tf_op jit(solution)/shard_map/psum | solution.py:90
  48.9 58.6 %reduce-scatter.2.cloned.1.call-done = f32[2,128,1024]{2,1,0:T(8,128)} async-done(((f32[2,1024,1024]{2,1,0:T(8,128)}), f32[2,128,1024]{2,1,0:T(8,128)}) %reduce-scatter.2.cloned.1.call-update) | async-done | bytes 1048592 | tf_op jit(solution)/shard_map/reduce_scatter | solution.py:112
  107.6 1.7 multiply_divide_fusion.1
  109.3 1.2 pad_maximum_fusion.1
  111.0 0.8 reduce.4
  112.4 3.4 all-to-all-start.1
  116.1 3.5 all-to-all-done.1
  119.6 44.8 %all-reduce.4.cloned.1.call-done = f32[2,1024,48]{1,2,0:T(8,128)} async-done(((f32[2,1024,48]{1,2,0:T(8,128)}), f32[2,1024,48]{1,2,0:T(8,128)}) %all-reduce.4.cloned.1.call-update) | async-done | bytes 393232 | tf_op jit(solution)/shard_map/psum | solution.py:90
  164.4 1.1 fusion.89
  165.9 81.2 %all-gather.2.cloned.1.call-done = f32[2,1024,1024]{2,1,0:T(8,128)} async-done(((f32[2,128,1024]{2,1,0:T(8,128)}), f32[2,1024,1024]{2,1,0:T(8,128)}) %all-gather.2.cloned.1.call-update) | async-done | bytes 8388624 | tf_op jit(solution)/shard_map/all_gather | solution.py:116
  247.1 6.5 %multiply_reduce_fusion.17 = (f32[60]{0:T(128)S(1)}, f32[1024,60]{0,1:T(8,128)S(1)}) fusion(f32[1024,60]{0,1:T(8,128)S(1)} %tile.16, f32[60]{0:T(128)S(1)} %mul.733, f32[2,1024,1024]{2,1,0:T(8,128)} %all-gather.2.cloned.1.call-done, s32[]{:T(128)S(6)} %select_n.49), kind=kOutput, calls=%fused_computation.123 | convolution fusion | flops 755220416 | bytes 4965108 | tf_op jit(solution)/shard_map/dot_general | solution.py:125
  253.9 6.5 %multiply_reduce_fusion.15 = (f32[60]{0:T(128)S(1)}, f32[1024,60]{0,1:T(8,128)S(1)}) fusion(f32[1024,60]{0,1:T(8,128)S(1)} %multiply_add_fusion.10, f32[60]{0:T(128)S(1)} %mul.733, f32[2,1024,1024]{2,1,0:T(8,128)} %all-gather.2.cloned.1.call-done, s32[]{:T(128)S(6)} %select_n.49), kind=kOutput, calls=%fused_computation.119 | convolution fusion | flops 755220416 | bytes 4965108 | tf_op jit(solution)/shard_map/dot_general | solution.py:125
  260.8 6.5 %multiply_reduce_fusion.13 = (f32[60]{0:T(128)S(1)}, f32[1024,60]{0,1:T(8,128)S(1)}) fusion(f32[1024,60]{0,1:T(8,128)S(1)} %multiply_add_fusion.9, f32[60]{0:T(128)S(1)} %mul.733, f32[2,1024,1024]{2,1,0:T(8,128)} %all-gather.2.cloned.1.call-done, s32[]{:T(128)S(6)} %select_n.49), kind=kOutput, calls=%fused_computation.115 | convolution fusion | flops 755220416 | bytes 4965108 | tf_op jit(solution)/shard_map/dot_general | solution.py:125
  267.6 6.7 %multiply_reduce_fusion.11 = (f32[60]{0:T(128)S(1)}, f32[1024,60]{0,1:T(8,128)S(1)}) fusion(f32[1024,60]{0,1:T(8,128)S(1)} %multiply_add_fusion.8, f32[60]{0:T(128)S(1)} %mul.733, f32[2,1024,1024]{2,1,0:T(8,128)} %all-gather.2.cloned.1.call-done, s32[]{:T(128)S(6)} %select_n.49), kind=kOutput, calls=%fused_computation.111 | convolution fusion | flops 755220416 | bytes 4965108 | tf_op jit(solution)/shard_map/dot_general | solution.py:125
  274.6 6.5 %multiply_reduce_fusion.9 = (f32[60]{0:T(128)S(1)}, f32[1024,60]{0,1:T(8,128)S(1)}) fusion(f32[1024,60]{0,1:T(8,128)S(1)} %multiply_add_fusion.7, f32[60]{0:T(128)S(1)} %mul.733, f32[2,1024,1024]{2,1,0:T(8,128)} %all-gather.2.cloned.1.call-done, s32[]{:T(128)S(6)} %select_n.49), kind=kOutput, calls=%fused_computation.107 | convolution fusion | flops 755220416 | bytes 4965108 | tf_op jit(solution)/shard_map/dot_general | solution.py:125
  281.4 6.5 %multiply_reduce_fusion.7 = (f32[60]{0:T(128)S(1)}, f32[1024,60]{0,1:T(8,128)S(1)}) fusion(f32[1024,60]{0,1:T(8,128)S(1)} %multiply_add_fusion.6, f32[60]{0:T(128)S(1)} %mul.733, f32[2,1024,1024]{2,1,0:T(8,128)} %all-gather.2.cloned.1.call-done, s32[]{:T(128)S(6)} %select_n.49), kind=kOutput, calls=%fused_computation.103 | convolution fusion | flops 755220416 | bytes 4965108 | tf_op jit(solution)/shard_map/dot_general | solution.py:125
  288.2 6.6 %multiply_reduce_fusion.5 = (f32[60]{0:T(128)S(1)}, f32[1024,60]{0,1:T(8,128)S(1)}) fusion(f32[1024,60]{0,1:T(8,128)S(1)} %multiply_add_fusion.5, f32[60]{0:T(128)S(1)} %mul.733, f32[2,1024,1024]{2,1,0:T(8,128)} %all-gather.2.cloned.1.call-done, s32[]{:T(128)S(6)} %select_n.49), kind=kOutput, calls=%fused_computation.99 | convolution fusion | flops 755220416 | bytes 4965108 | tf_op jit(solution)/shard_map/dot_general | solution.py:125
  295.2 7.0 %multiply_reduce_fusion.3 = (f32[60]{0:T(128)S(1)}, f32[1024,60]{0,1:T(8,128)S(1)}) fusion(f32[1024,60]{0,1:T(8,128)S(1)} %multiply_add_fusion.4, f32[60]{0:T(128)S(1)} %mul.733, f32[2,1024,1024]{2,1,0:T(8,128)} %all-gather.2.cloned.1.call-done, s32[]{:T(128)S(6)} %select_n.49), kind=kOutput, calls=%fused_computation.95 | convolution fusion | flops 755220416 | bytes 4965108 | tf_op jit(solution)/shard_map/dot_general | solution.py:125
  302.6 6.5 %multiply_reduce_fusion.1 = (f32[60]{0:T(128)S(1)}, f32[1024,60]{0,1:T(8,128)S(1)}) fusion(f32[1024,60]{0,1:T(8,128)S(1)} %multiply_add_fusion.3, f32[60]{0:T(128)S(1)} %mul.733, f32[2,1024,1024]{2,1,0:T(8,128)} %all-gather.2.cloned.1.call-done, s32[]{:T(128)S(6)} %select_n.49), kind=kOutput, calls=%fused_computation.91 | convolution fusion | flops 755220416 | bytes 4965108 | tf_op jit(solution)/shard_map/dot_general | solution.py:125
  309.3 4.3 %fusion.67 = f32[60]{0:T(128)S(1)} fusion(f32[2,1024,1024]{2,1,0:T(8,128)S(1)} %bitcast.162, s32[]{:T(128)S(6)} %select_n.49, f32[1024,60]{0,1:T(8,128)S(1)} %get-tuple-element.23, f32[1024,60]{0,1:T(8,128)S(1)} %multiply_add_fusion.3, f32[60]{0:T(128)S(1)} %div.291, f32[60]{0:T(128)S(1)} %mul.733), kind=kOutput, calls=%fused_computation.56 | convolution fusion | flops 755466176 | bytes 5244660 | tf_op jit(solution)/shard_map/dot_general | solution.py:125
  313.9 17.7 %all_gather.7 = bf16[8,1024,5,12]{1,3,2,0:T(8,128)(2,1)S(1)} all-gather(bf16[1,1024,5,12]{1,3,2,0:T(8,128)(2,1)S(1)} %broadcast_in_dim_reshape.2), channel_id=1, replica_groups=mesh['groups'=2,'people'=4,'blocks'=2,'sub'=2] {'people','sub'}, dimensions={0}, use_global_device_ids=true | all-gather | bytes 1105920 | tf_op jit(solution)/shard_map/all_gather | solution.py:131
  331.6 1.0 copy.84
  332.7 1.6 fusion.149
  338.0 3.4 all-to-all-start
  341.6 5.1 %all-to-all-done = bf16[1,256,5,48]{1,2,0,3:T(8,128)(2,1)S(1)} async-done(((bf16[1,256,5,48]{1,2,0,3:T(8,128)(2,1)}), bf16[1,256,5,48]{1,2,0,3:T(8,128)(2,1)S(1)}, u32[]{:S(2)}, u32[]{:S(2)}) %all-to-all-start) | async-done | bytes 122912 | tf_op jit(solution)/shard_map/all_to_all | solution.py:145
  347.3 18.9 %all-reduce.1 = (f32[12,10,10]{2,1,0:T(8,128)S(1)}, f32[12,10]{1,0:T(8,128)S(1)}) all-reduce(f32[12,10,10]{2,1,0:T(8,128)S(1)} %fusion.94, f32[12,10]{1,0:T(8,128)S(1)} %bitcast.176), channel_id=1, replica_groups=mesh['groups'=2,'people'=4,'blocks'=2,'sub'=2] {'people'}, use_global_device_ids=true, to_apply=%region_33.34 | all-reduce | flops 1320 | bytes 10560 | tf_op jit(solution)/shard_map/psum | solution.py:162
  369.3 0.7 copy.65
  (117 shorter events, 14.8 us)
Async XLA Ops:
  6.5 101.0 %reduce-scatter.2.cloned.1.call-start = ((), (), s32[]{:S(2)}) async-start(), calls=%async_computation.4 | async-start | bytes 9437184 | tf_op jit(solution)/shard_map/reduce_scatter | solution.py:112
  14.6 0.7 copy-start
  14.7 101.3 %copy-start.1 = (f32[5]{0:T(128)S(1)}, f32[5]{0:T(128)}, u32[]{:S(2)}) copy-start(f32[5]{0:T(128)} %param.7) | copy-start | bytes 64
  14.7 149.7 %all-reduce.4.cloned.1.call-start = ((), (), s32[]{:S(2)}) async-start(), calls=%async_computation.3 | async-start | bytes 786432 | tf_op jit(solution)/shard_map/psum | solution.py:90
  16.7 230.4 %all-gather.2.cloned.1.call-start = ((), (), s32[]{:S(2)}) async-start(), calls=%async_computation.5 | async-start | bytes 9437184 | tf_op jit(solution)/shard_map/all_gather | solution.py:116
  112.4 7.1 %all-to-all-start.1 = ((bf16[4,2,1536]{2,1,0:T(2,128)(2,1)}), bf16[4,2,1536]{2,1,0:T(2,128)(2,1)S(1)}, u32[]{:S(2)}, u32[]{:S(2)}) async-start(bf16[4,2,1536]{2,1,0:T(2,128)(2,1)} %reshape.722), calls=%async_computation.2 | async-start | bytes 49152 | tf_op jit(solution)/shard_map/all_to_all | solution.py:146
  288.2 21.0 %slice-start = ((s8[8388608]{0:T(1024)(128)(4,1)}), s8[4194304]{0:T(1024)(128)(4,1)S(1)}, s32[]{:S(2)}) async-start(s8[8388608]{0:T(1024)(128)(4,1)} %bitcast.161), calls=%async_computation.6 | async-start | bytes 8388608
  295.2 14.1 %slice-start.1 = ((s8[8388608]{0:T(1024)(128)(4,1)}), s8[4194304]{0:T(1024)(128)(4,1)S(1)}, s32[]{:S(2)}) async-start(s8[8388608]{0:T(1024)(128)(4,1)} %bitcast.161), calls=%async_computation.7 | async-start | bytes 8388608
  338.0 8.6 %all-to-all-start = ((bf16[1,256,5,48]{1,2,0,3:T(8,128)(2,1)}), bf16[1,256,5,48]{1,2,0,3:T(8,128)(2,1)S(1)}, u32[]{:S(2)}, u32[]{:S(2)}) async-start(bf16[1,256,5,48]{1,2,0,3:T(8,128)(2,1)} %copy.56), calls=%async_computation.1 | async-start | bytes 393216 | tf_op jit(solution)/shard_map/all_to_all | solution.py:145
Sparse Core Ops, SparseCore 0:
  14.8 92.7 reduce-scatter.1
  109.9 54.4 all-reduce.3
  166.0 81.0 all-gather.1
where the time goes:
time: 381 us; the launch traced here: 377 us
  waiting for transfers between devices  193 us (51%)
  matrix products  69.5 us (18%)
  blocking collectives  68.3 us (18%)
  other arithmetic  16.9 us (4%)
  between operations  13.9 us (4%)
  local copies, waits for them, and re-layouts  8.04 us (2%)
  starting transfers between devices  6.88 us (2%)
    all_gather x1, waiting for transfers between devices, shards(): whole = lax.all_gather(systems, ('people', 'sub'), axis=1, tiled=True)  81.2 us
    dot_general x10, matrix products, shards(): jnp.dot(system, direction, precision=highest) + shifts * direction  63.4 us
    reduce_scatter x1, waiting for transfers between devices, shards(): lax.psum_scatter(gram_stack, ('people', 'sub'), scatter_dimension=1, tile...  58.6 us
    psum x1, waiting for transfers between devices, shards(): lax.psum((jnp.stack(sums), jnp.stack(squares), jnp.stack(cross), jnp.stac...  44.8 us
    psum x1, blocking collectives, shards(): lax.psum((jnp.stack(sums), jnp.stack(squares), jnp.stack(cross), jnp.stac...  31.7 us
    psum x1, blocking collectives, shards(): gram_two, cross_two = lax.psum((gram_two, cross_two), 'people')  18.9 us
    all_gather x1, blocking collectives, shards(): lax.all_gather(scaled[None], ('people', 'sub'), axis=0, tiled=True)  17.7 us
  transfers between devices with their start and end apart: 5, of which 5 were waited for; matrix products, arithmetic and copies ran while one was open for 2% of the time, Pallas kernels for 0%

commit v1 on v0

v1 whole, which is shorter than its diff:
```python
import functools

import jax
import jax.numpy as jnp
from jax import lax
from jax.experimental import pallas as pl
from jax.experimental.pallas import tpu as pltpu
from jax.sharding import PartitionSpec as P

TRAITS = 48
RIDGES = 5
FOLDS = 2
ITERS = 10
ITERS_TWO = 4

f32 = jnp.float32
bf16 = jnp.bfloat16
highest = lax.Precision.HIGHEST
natural = (((1,), (0,)), ((), ()))
transposed = (((1,), (1,)), ((), ()))


def round_up(value, step):
    return -(-value // step) * step


def split_high_low(value):
    high = value.astype(bf16)
    return high, (value - high.astype(f32)).astype(bf16)


def iota(shape, axis):
    return lax.broadcasted_iota(jnp.int32, shape, axis)


def count_steps(index, step, most):
    return sum([(index >= step * (turn + 1)).astype(jnp.int32) for turn in range(most)])


def pack_kernel(dosage_ref, fold_ref, pheno_ref, packed_ref, tail_ref):
    row_count, block_size = dosage_ref.shape
    trait_count = pheno_ref.shape[0]
    centred = (dosage_ref[...] - 100).astype(f32)
    packed_ref[:block_size, :] = centred.T.astype(bf16)
    packed_ref[block_size : block_size + trait_count, :] = pheno_ref[...]
    tail_ref[...] = jnp.zeros_like(tail_ref)
    tail_ref[0:1, :] = fold_ref[...].astype(f32)
    rest = jnp.sum(centred * centred, 0, keepdims=True)
    place = 1
    for piece in range(3):
        part = rest.astype(bf16).astype(f32)
        rest = rest - part
        for start in range(0, block_size, row_count):
            tail_ref[place : place + 1, :] = part[:, start : start + row_count]
            place += 1
    packed_ref[block_size + trait_count :, :] = tail_ref[...].astype(bf16)


def fold_sign(place, first_host, host_count):
    if host_count != 2:
        return 1
    return jnp.where(place <= first_host, 1, -1)


def quarter_of(turn, place, first_host, host_count, people_count):
    return lax.rem(
        place + fold_sign(place, first_host, host_count) * turn + people_count, people_count
    )


def start_copies(chunks, people_ref, sems, starts):
    copies = []
    for index, (chunk, start) in enumerate(zip(chunks, starts)):
        width = chunk.shape[1]
        copies.append(
            pltpu.make_async_copy(
                chunk,
                people_ref.at[:, pl.ds(pl.multiple_of(start, width), width)],
                sems.at[index],
            )
        )
    for copy in copies:
        copy.start()
    return copies


def base_traits(quarter, part_rows, host, trait_group):
    row = iota((2 * part_rows, TRAITS), 0)
    part = (row >= part_rows).astype(jnp.int32)
    place = row - part_rows * part
    place = place - quarter * count_steps(place, quarter, -(-part_rows // quarter))
    return place + quarter * part + host * trait_group


def masked_targets(people_ref, block_size, lanes, core, choose):
    own = people_ref[block_size + TRAITS :, lanes].astype(f32)[0:1, :] == core.astype(f32)
    train = jnp.where(own, 0.0, 1.0)
    targets = lax.dot_general(
        choose,
        people_ref[block_size : block_size + TRAITS, lanes],
        natural,
        preferred_element_type=f32,
    )
    return targets * train, train


def fill_left(people_ref, left_ref, block_size, lanes, core, choose):
    targets, train = masked_targets(people_ref, block_size, lanes, core, choose)
    width = train.shape[1]
    left_ref[:block_size, :] = people_ref[:block_size, lanes] * train.astype(bf16)
    rows = targets.shape[0]
    left_ref[block_size : block_size + rows, :] = targets.astype(bf16)
    left_ref[block_size + rows :, :] = jnp.where(iota((16, width), 0) == 0, train, 1.0).astype(
        bf16
    )


def left_slabs(total):
    half = round_up(total // 2, 16)
    return [(0, half), (half, total)]


def early_kernel(sizes, *refs):
    block_size, row_count, trait_group, quarter, part_rows, first_host, host_count, _ = sizes
    chunks, (gram_ref, pheno_ref, people_ref, left_ref, sems) = refs[:4], refs[4:]
    core = lax.axis_index("sub")
    host = jnp.clip(lax.axis_index("people") - first_host, 0, host_count - 1)
    starts = [
        (2 * turn + (core if side == 0 else 1 - core)) * row_count
        for turn in range(2)
        for side in range(2)
    ]
    copies = start_copies(chunks, people_ref, sems, starts)
    for copy in copies:
        copy.wait()
    choose = (
        iota((2 * part_rows, TRAITS), 1) == base_traits(quarter, part_rows, host, trait_group)
    ).astype(bf16)
    fill_left(people_ref, left_ref, block_size, slice(None), core, choose)
    for start, stop in left_slabs(left_ref.shape[0]):
        gram_ref[start:stop, :] = lax.dot_general(
            left_ref[start:stop, :],
            people_ref[:block_size, :],
            transposed,
            preferred_element_type=f32,
        )
    first = lax.axis_index("blocks") * (2 * quarter) + core * quarter
    pick = iota((16, TRAITS), 1) == iota((16, TRAITS), 0) + first
    pheno_ref[...] = lax.dot_general(
        pick.astype(bf16),
        people_ref[block_size : block_size + TRAITS, : 2 * row_count],
        natural,
        preferred_element_type=f32,
    ).astype(bf16)


def fit_kernel(sizes, rows, ridges_ref, early_ref, *refs):
    (
        block_size, row_count, trait_group, quarter, part_rows, first_host, host_count, people_count,
    ) = sizes
    chunk_count = people_count * 2
    chunks = refs[:chunk_count]
    keep_ref, send_ref = refs[chunk_count : chunk_count + 2]
    (
        people_ref,
        left_ref,
        gram_ref,
        high_ref,
        low_ref,
        column_ref,
        history_ref,
        direction_ref,
        split_ref,
        alpha_ref,
        beta_ref,
        tall_ref,
        predict_ref,
        sems,
        early_sem,
    ) = refs[chunk_count + 2 :]
    core = lax.axis_index("sub")
    place = lax.axis_index("people")
    host = jnp.clip(place - first_host, 0, host_count - 1)
    people = chunk_count * row_count
    train_count = people - people // FOLDS
    width = 2 * row_count
    base_rows = 2 * part_rows
    starts = []
    for turn in range(people_count):
        where = quarter_of(turn, place, first_host, host_count, people_count)
        for side in range(2):
            starts.append(where * width + (core if side == 0 else 1 - core) * row_count)
    early_copy = pltpu.make_async_copy(early_ref, gram_ref, early_sem)
    early_copy.start()
    copies = start_copies(chunks, people_ref, sems, starts)
    for copy in copies[2 : chunk_count - 2]:
        copy.wait()
    choose = (
        iota((base_rows, TRAITS), 1) == base_traits(quarter, part_rows, host, trait_group)
    ).astype(bf16)
    early_copy.wait()

    def late(turn, carry):
        where = quarter_of(turn, place, first_host, host_count, people_count)
        lanes = pl.ds(pl.multiple_of(where * width, width), width)
        fill_left(people_ref, left_ref, block_size, lanes, core, choose)
        for start, stop in left_slabs(left_ref.shape[0]):
            gram_ref[start:stop, :] += lax.dot_general(
                left_ref[start:stop, :],
                people_ref[:block_size, lanes],
                transposed,
                preferred_element_type=f32,
            )
        return carry

    lax.fori_loop(1, people_count - 1, late, 0, unroll=people_count <= 4)
    for copy in copies[:2] + copies[chunk_count - 2 :]:
        copy.wait()

    tail = people_ref[block_size + TRAITS :, :].astype(f32)
    own = tail[0:1, :] == core.astype(f32)
    square_parts = []
    pieces_per = block_size // row_count
    for piece in range(pieces_per):
        part = jnp.zeros((1, row_count), f32)
        for chunk in range(chunk_count):
            lanes = slice(chunk * row_count, (chunk + 1) * row_count)
            for level in range(3):
                line = 1 + level * pieces_per + piece
                part = part + tail[line : line + 1, lanes]
        square_parts.append(part)
    squares = jnp.concatenate(square_parts, 1)
    targets, _ = masked_targets(people_ref, block_size, slice(None), core, choose)
    totals = jnp.sum(targets, 1, keepdims=True)
    train_sums = gram_ref[block_size + base_rows : block_size + base_rows + 1, :]
    mean = gram_ref[block_size + base_rows + 1 : block_size + base_rows + 2, :] / people
    spread = jnp.sqrt(squares / people - mean * mean + 1e-05)
    inverse = 1.0 / spread
    offset_sums = train_sums - (0.5 * train_count) * mean
    shares = inverse * (1.0 / train_count)
    column_ref[...] = jnp.concatenate([mean, offset_sums, shares] + [mean] * 5, 0).T

    slab = 64

    def assemble(turn, carry):
        span = pl.ds(pl.multiple_of(turn * slab, slab), slab)
        columns = column_ref[span, :]
        system = (
            (gram_ref[span, :] - columns[:, 1:2] * mean - columns[:, 0:1] * offset_sums)
            * columns[:, 2:3]
            * inverse
        )
        high, low = split_high_low(system)
        high_ref[span, :] = high
        low_ref[span, :] = low
        return carry

    lax.fori_loop(0, block_size // slab, assemble, 0)

    right = (gram_ref[block_size : block_size + base_rows, :] - totals * mean) * shares
    smallest = ridges_ref[0]
    for ridge in range(1, RIDGES):
        smallest = jnp.minimum(smallest, ridges_ref[ridge])
    history_ref[:base_rows, :] = right
    direction_ref[...] = right
    high, low = split_high_low(right)
    split_ref[:base_rows, :] = high
    split_ref[base_rows:, :] = low

    def step(turn, current):
        both = lax.dot_general(
            split_ref[...], high_ref[...], natural, preferred_element_type=f32
        )
        other = lax.dot_general(
            split_ref[:base_rows, :], low_ref[...], natural, preferred_element_type=f32
        )
        direction = direction_ref[...]
        image = both[:base_rows, :] + (both[base_rows:, :] + other) + smallest * direction
        alpha = current / jnp.sum(direction * image, 1, keepdims=True)
        residual = (
            history_ref[pl.ds(pl.multiple_of(turn * base_rows, base_rows), base_rows), :]
            - alpha * image
        )
        following = jnp.sum(residual * residual, 1, keepdims=True)
        beta = following / current
        direction = residual + beta * direction
        history_ref[
            pl.ds(pl.multiple_of((turn + 1) * base_rows, base_rows), base_rows), :
        ] = residual
        direction_ref[...] = direction
        high, low = split_high_low(direction)
        split_ref[:base_rows, :] = high
        split_ref[base_rows:, :] = low
        alpha_ref[pl.ds(pl.multiple_of(turn * base_rows, base_rows), base_rows), :] = alpha
        beta_ref[pl.ds(pl.multiple_of(turn * base_rows, base_rows), base_rows), :] = beta
        return following

    lax.fori_loop(0, ITERS, step, jnp.sum(right * right, 1, keepdims=True))

    lane = iota((1, 128), 1)
    extra = jnp.zeros((1, 128), f32)
    for ridge in range(RIDGES):
        extra = jnp.where(lane == ridge, ridges_ref[ridge] - smallest, extra)
    ratio = jnp.ones((base_rows, 128), f32)
    scale = ratio
    link = jnp.zeros((base_rows, 1), f32)
    scales, alphas, betas = [], [], []
    for turn in range(ITERS):
        span = slice(turn * base_rows, (turn + 1) * base_rows)
        alpha, beta = alpha_ref[span, :], beta_ref[span, :]
        ratio = 1.0 / (1.0 + extra * alpha + (alpha * link) * (1.0 - ratio))
        scales.append(scale)
        alphas.append(alpha * ratio)
        betas.append(beta * ratio * ratio)
        scale = scale * ratio
        link = beta / alpha
    reach = alphas[-1]
    factors = [scales[-1] * reach]
    for turn in range(ITERS - 2, -1, -1):
        reach = alphas[turn] + betas[turn] * reach
        factors.append(scales[turn] * reach)
    factors = factors[::-1]
    for ridge in range(RIDGES):
        for start in range(0, base_rows, 16):
            fit = jnp.zeros((16, block_size), f32)
            for turn in range(ITERS):
                line = turn * base_rows + start
                fit = (
                    fit
                    + factors[turn][start : start + 16, ridge : ridge + 1]
                    * history_ref[line : line + 16, :]
                )
            line = ridge * base_rows + start
            tall_ref[line : line + 16, :] = (fit * inverse).astype(bf16)

    tall_count = RIDGES * base_rows
    row = iota((2 * rows, tall_count), 0)
    part = (row >= rows).astype(jnp.int32)
    line = row - rows * part
    ridge = jnp.minimum(count_steps(line, quarter, RIDGES), RIDGES - 1)
    source = ridge * base_rows + part * part_rows + (line - quarter * ridge)
    source = jnp.where(line < quarter * RIDGES, source, 0)
    pack = (iota((2 * rows, tall_count), 1) == source).astype(bf16)
    scaled = lax.dot_general(pack, tall_ref[...], natural, preferred_element_type=f32)
    offset = jnp.sum(scaled * mean, 1, keepdims=True)
    scaled = scaled.astype(bf16)

    def predict(lanes, own):
        outcome = lax.dot_general(
            scaled, people_ref[:block_size, lanes], natural, preferred_element_type=f32
        )
        predict_ref[:, lanes] = jnp.where(own, outcome - offset, 0.0).astype(bf16)

    if people_count <= 4:
        predict(slice(None), own)
    else:

        def predict_part(turn, carry):
            lanes = pl.ds(pl.multiple_of(turn * width, width), width)
            lines = people_ref[block_size + TRAITS :, lanes].astype(f32)
            predict(lanes, lines[0:1, :] == core.astype(f32))
            return carry

        lax.fori_loop(0, people_count, predict_part, 0)
    keep_ref[...] = predict_ref[pl.ds(pl.multiple_of(core * rows, rows), rows), :]
    send_ref[...] = predict_ref[pl.ds(pl.multiple_of((1 - core) * rows, rows), rows), :]


def join_kernel(sizes, keep_ref, received_ref, *piece_refs):
    first_host, host_count, people_count = sizes
    place = lax.axis_index("people")
    width = piece_refs[0].shape[1]
    for turn, piece_ref in enumerate(piece_refs):
        where = quarter_of(turn, place, first_host, host_count, people_count)
        lanes = pl.ds(pl.multiple_of(where * width, width), width)
        piece_ref[...] = (
            keep_ref[:, lanes].astype(f32) + received_ref[:, lanes].astype(f32)
        ).astype(bf16)


def split_index(index, quarter, rows, block_count):
    block = count_steps(index, rows, block_count - 1)
    place = index - rows * block
    ridge = count_steps(place, quarter, RIDGES)
    return block * RIDGES + ridge, place - quarter * ridge, ridge < RIDGES


def moment_kernel(sizes, pheno_ref, *refs):
    quarter, rows, block_count, stat_rows = sizes
    pieces, sums_ref = refs[:-1], refs[-1]
    width = block_count * rows
    predictors = jnp.concatenate([piece[...] for piece in pieces], 0)
    slot, trait, live = split_index(iota((1, width), 1), quarter, rows, block_count)
    _, row_trait, row_live = split_index(iota((width, 1), 0), quarter, rows, block_count)
    gram = lax.dot_general(predictors, predictors, transposed, preferred_element_type=f32)
    gram = jnp.where((row_trait == trait) & row_live & live, gram, 0.0)
    pick = (iota((stat_rows, width), 0) == slot) & live
    table = lax.dot_general(
        pick.astype(f32), gram, natural, precision=highest, preferred_element_type=f32
    )
    cross = lax.dot_general(pheno_ref[...], predictors, transposed, preferred_element_type=f32)
    chosen = (iota((16, width), 0) == trait) & live
    cross = jnp.sum(jnp.where(chosen, cross, 0.0), 0, keepdims=True)
    sums_ref[...] = jnp.where(iota((stat_rows, width), 0) == stat_rows - 1, cross, table)


def second_kernel(sizes, ridges_ref, *refs):
    people, quarter, rows, block_count, stat_rows, part_count = sizes
    parts = refs[:part_count]
    pieces = refs[part_count : part_count + block_count]
    out_ref = refs[-1]
    width = block_count * rows
    slots = block_count * RIDGES
    table = parts[0][...]
    for part in parts[1:]:
        table = table + part[...]
    table = table * (1.0 / people)
    slot, trait, live = split_index(iota((1, width), 1), quarter, rows, block_count)
    _, row_trait, row_live = split_index(iota((width, 1), 0), quarter, rows, block_count)
    out_lane = iota((1, 128), 1)
    out_ridge = count_steps(out_lane, 16, 7)
    out_trait = out_lane - 16 * out_ridge
    out_live = (out_trait < quarter) & (out_ridge < RIDGES)
    expand = ((row_trait == out_trait) & row_live & out_live).astype(f32)
    stacked = jnp.concatenate(
        [jnp.where((slot == index) & live, table, 0.0) for index in range(slots)], 0
    )
    wide = lax.dot_general(
        stacked, expand, natural, precision=highest, preferred_element_type=f32
    )
    sublane = iota((stat_rows, 128), 0)
    columns = []
    residual = jnp.zeros((stat_rows, 128), f32)
    trace = jnp.zeros((stat_rows, 128), f32)
    for index in range(slots):
        column = wide[index * stat_rows : (index + 1) * stat_rows, :]
        here = sublane == index
        residual = jnp.where(here, column[stat_rows - 1 : stat_rows, :], residual)
        column = jnp.where(sublane < slots, column, 0.0)
        trace = jnp.where(here, column, trace)
        columns.append(column)
    level = jnp.sum(trace, 0, keepdims=True) / slots + 1e-06
    ridge = jnp.zeros((1, 128), f32)
    for index in range(RIDGES):
        ridge = jnp.where(out_ridge == index, ridges_ref[index], ridge)
    level_shift = ridge * level
    direction = residual
    weights = jnp.zeros_like(residual)
    current = jnp.sum(residual * residual, 0, keepdims=True)
    for step in range(ITERS_TWO):
        image = level_shift * direction
        for index in range(slots):
            image = image + columns[index] * direction[index : index + 1, :]
        alpha = current / jnp.sum(direction * image, 0, keepdims=True)
        weights = weights + alpha * direction
        residual = residual - alpha * image
        following = jnp.sum(residual * residual, 0, keepdims=True)
        direction = residual + following / current * direction
        current = following
    weights = jnp.where(out_live, weights, 0.0)
    turned = weights.T
    pick = (iota((stat_rows, width), 0) == slot) & live
    tall = lax.dot_general(
        turned, pick.astype(f32), natural, precision=highest, preferred_element_type=f32
    )
    row = iota((128, 1), 0)
    tall = jnp.where(row - 16 * count_steps(row, 16, 7) == trait, tall, 0.0)
    tall = tall[: RIDGES * 16, :]
    high, low = split_high_low(tall)
    predictors = jnp.concatenate([piece[...] for piece in pieces], 0)
    both = lax.dot_general(
        jnp.concatenate([high, low], 0), predictors, natural, preferred_element_type=f32
    )
    answer = both[: RIDGES * 16, :] + both[RIDGES * 16 :, :]
    for ridge in range(RIDGES):
        out_ref[ridge] = answer[ridge * 16 : ridge * 16 + quarter, :]


def whole(count):
    return [pl.BlockSpec(memory_space=pltpu.VMEM)] * count


def anywhere(count):
    return [pl.BlockSpec(memory_space=pl.ANY)] * count


def shards(dosage, fold, pheno, ridges):
    row_count, block_size = dosage.shape
    people_count = lax.axis_size("people")
    block_count = lax.axis_size("blocks")
    people = row_count * people_count * 2
    host_count = block_count
    first_host = people_count // 2 - host_count // 2
    hosts = [first_host + host for host in range(host_count)]
    trait_group = TRAITS // host_count
    quarter = trait_group // 2
    rows = round_up(quarter * RIDGES, 16)
    part_rows = round_up(quarter, 16)
    base_rows = 2 * part_rows
    tail_rows = round_up(1 + 3 * (block_size // row_count), 16)
    packed_rows = block_size + TRAITS + tail_rows
    left_rows = block_size + base_rows + 16
    width = 2 * row_count

    packed = pl.pallas_call(
        pack_kernel,
        out_shape=jax.ShapeDtypeStruct((packed_rows, row_count), bf16),
        in_specs=whole(3),
        out_specs=whole(1)[0],
        scratch_shapes=[pltpu.VMEM((tail_rows, row_count), f32)],
        name="pack",
    )(dosage, fold[None, :], pheno.T)

    def swap(value):
        return lax.ppermute(value, "sub", [(0, 1), (1, 0)])

    def source_of(host, turn):
        mirrored = host_count == 2 and host > first_host
        return (host - turn if mirrored else host + turn) % people_count

    order = [turn for turn in range(2, people_count - 1)] + [1, people_count - 1]
    received = {0: packed}
    for turn in order:
        received[turn] = lax.ppermute(
            packed, "people", [(source_of(host, turn), host) for host in hosts]
        )
    swapped = {turn: swap(received[turn]) for turn in [0, people_count - 1] + order[:-1]}
    chunks = []
    for turn in range(people_count):
        chunks += [received[turn], swapped[turn]]

    sizes = (
        block_size, row_count, trait_group, quarter, part_rows, first_host, host_count, people_count,
    )
    early, pheno_quarter = pl.pallas_call(
        functools.partial(early_kernel, sizes),
        out_shape=[
            jax.ShapeDtypeStruct((left_rows, block_size), f32),
            jax.ShapeDtypeStruct((16, width), bf16),
        ],
        in_specs=anywhere(4),
        out_specs=whole(2),
        scratch_shapes=[
            pltpu.VMEM((packed_rows, 2 * width), bf16),
            pltpu.VMEM((left_rows, 2 * width), bf16),
            pltpu.SemaphoreType.DMA((4,)),
        ],
        cost_estimate=pl.CostEstimate(
            flops=4 * left_rows * block_size * width,
            bytes_accessed=8 * left_rows * block_size,
            transcendentals=0,
        ),
        name="early",
    )(*chunks[:2], *chunks[-2:])
    keep, send = pl.pallas_call(
        functools.partial(fit_kernel, sizes, rows),
        out_shape=[jax.ShapeDtypeStruct((rows, people), bf16)] * 2,
        in_specs=[pl.BlockSpec(memory_space=pltpu.SMEM)] + anywhere(1 + len(chunks)),
        out_specs=whole(2),
        scratch_shapes=[
            pltpu.VMEM((packed_rows, people), bf16),
            pltpu.VMEM((left_rows, width), bf16),
            pltpu.VMEM((left_rows, block_size), f32),
            pltpu.VMEM((block_size, block_size), bf16),
            pltpu.VMEM((block_size, block_size), bf16),
            pltpu.VMEM((block_size, 8), f32),
            pltpu.VMEM(((ITERS + 1) * base_rows, block_size), f32),
            pltpu.VMEM((base_rows, block_size), f32),
            pltpu.VMEM((2 * base_rows, block_size), bf16),
            pltpu.VMEM((ITERS * base_rows, 1), f32),
            pltpu.VMEM((ITERS * base_rows, 1), f32),
            pltpu.VMEM((RIDGES * base_rows, block_size), bf16),
            pltpu.VMEM((2 * rows, people), bf16),
            pltpu.SemaphoreType.DMA((len(chunks),)),
            pltpu.SemaphoreType.DMA,
        ],
        name="fit",
    )(ridges, early, *chunks)

    pieces = pl.pallas_call(
        functools.partial(join_kernel, (first_host, host_count, people_count)),
        out_shape=[jax.ShapeDtypeStruct((rows, width), bf16)] * people_count,
        in_specs=whole(2),
        out_specs=whole(people_count),
        name="join",
    )(keep, swap(send))
    arrived = {0: pieces[0]}
    for turn in order:
        arrived[turn] = lax.ppermute(
            pieces[turn], "people", [(host, source_of(host, turn)) for host in hosts]
        )

    place = lax.axis_index("people")
    block = lax.axis_index("blocks")

    def piece_for(target):
        turn = place - first_host - target
        if host_count == 2:
            turn = jnp.where(target == 1, -turn, turn)
        turn = turn % people_count
        chosen = arrived[0]
        for other in range(1, people_count):
            chosen = jnp.where(turn == other, arrived[other], chosen)
        return chosen

    parts = [piece_for(block)]
    for turn in range(1, block_count):
        parts.append(
            lax.ppermute(
                piece_for((block + turn) % block_count),
                "blocks",
                [(source, (source + turn) % block_count) for source in range(block_count)],
            )
        )

    stat_rows = round_up(block_count * RIDGES + 1, 8)
    table_width = block_count * rows
    sums = pl.pallas_call(
        functools.partial(moment_kernel, (quarter, rows, block_count, stat_rows)),
        out_shape=jax.ShapeDtypeStruct((stat_rows, table_width), f32),
        in_specs=whole(1 + block_count),
        out_specs=whole(1)[0],
        name="moment",
    )(pheno_quarter, *parts)
    tables = [sums]
    for turn in order:
        tables.append(
            lax.ppermute(
                sums,
                "people",
                [(source, (source + turn) % people_count) for source in range(people_count)],
            )
        )
    answer = pl.pallas_call(
        functools.partial(
            second_kernel, (people, quarter, rows, block_count, stat_rows, people_count)
        ),
        out_shape=jax.ShapeDtypeStruct((RIDGES, quarter, width), f32),
        in_specs=[pl.BlockSpec(memory_space=pltpu.SMEM)] + whole(people_count + block_count),
        out_specs=whole(1)[0],
        name="second",
    )(ridges, *tables, *parts)
    return answer.transpose(1, 0, 2)


def solution(mesh):
    return jax.shard_map(
        shards,
        mesh=mesh,
        in_specs=(
            P(("groups", "people", "sub"), "blocks"),
            P(("groups", "people", "sub")),
            P(("groups", "people", "sub"), None),
            P(),
        ),
        out_specs=P(("blocks", "sub"), None, ("groups", "people")),
        check_vma=False,
    )
```

time: 381 us -> 98.9 us (0.26)
  waiting for transfers between devices: 193 us -> 31.7 us
  matrix products: 69.5 us -> 0 us
  blocking collectives: 68.3 us -> 0 us
  Pallas kernels: 0 us -> 36.9 us
  starting transfers between devices: 6.88 us -> 23.1 us
  other arithmetic: 16.9 us -> 1.47 us
  between operations: 13.9 us -> 0.22 us
    all_gather x1 -> x0, waiting for transfers between devices: 81.2 us -> none  [shards(): whole = lax.all_gather(systems, ('people', 'sub'), axis=1, tiled=True)]
    dot_general x25 -> x0, matrix products: 69.5 us -> none  [the longest x10 63.4 us: shards(): jnp.dot(system, direction, precision=highest) + shifts * direction]
    reduce_scatter x1 -> x0, waiting for transfers between devices: 58.6 us -> none  [shards(): lax.psum_scatter(gram_stack, ('people', 'sub'), scatter_dimension=1, tile...]
    psum x2 -> x0, blocking collectives: 50.6 us -> none  [the longest x1 31.7 us: shards(): lax.psum((jnp.stack(sums), jnp.stack(squares), jnp.stack(cross), jnp.stac...]
    psum x1 -> x0, waiting for transfers between devices: 44.8 us -> none  [shards(): lax.psum((jnp.stack(sums), jnp.stack(squares), jnp.stack(cross), jnp.stac...]
    pallas_call x0 -> x6, Pallas kernels: none -> 36.9 us  [the longest x1 22.4 us: shards(): pl.pallas_call(functools.partial(fit_kernel, sizes, rows), out_shape=[jax...]
    ppermute x0 -> x15, waiting for transfers between devices: none -> 31.7 us  [the longest x3 18.9 us: shards(): lax.ppermute(packed, 'people', [(source_of(host, turn), host) for host in...]
    ppermute x0 -> x15, starting transfers between devices: none -> 23.1 us  [the longest x3 9.64 us: shards(): lax.ppermute(packed, 'people', [(source_of(host, turn), host) for host in...]
  transfers between devices with their start and end apart: 5 -> 15, of which waited for: 5 -> 7; matrix products, arithmetic and copies ran while one was open for 2% -> 0% of each run, Pallas kernels for 0% -> 6%
where the time goes in v1:
time: 98.9 us; the launch traced here: 98.4 us
  Pallas kernels  36.9 us (37%)
  waiting for transfers between devices  31.7 us (32%)
  starting transfers between devices  23.1 us (23%)
  local copies, waits for them, and re-layouts  4.99 us (5%)
  other arithmetic  1.47 us (1%)
    pallas_call x1, Pallas kernels, shards(): pl.pallas_call(functools.partial(fit_kernel, sizes, rows), out_shape=[jax...  22.4 us
    ppermute x3, waiting for transfers between devices, shards(): lax.ppermute(packed, 'people', [(source_of(host, turn), host) for host in...  18.9 us
    ppermute x3, starting transfers between devices, shards(): lax.ppermute(packed, 'people', [(source_of(host, turn), host) for host in...  9.64 us
    ppermute x3, starting transfers between devices, shards(): lax.ppermute(sums, 'people', [(source, (source + turn) % people_count) fo...  7.6 us
    ppermute x3, waiting for transfers between devices, shards(): lax.ppermute(pieces[turn], 'people', [(host, source_of(host, turn)) for h...  6.88 us
    pallas_call x1, Pallas kernels, shards(): pl.pallas_call(functools.partial(early_kernel, sizes), out_shape=[jax.Sha...  6.13 us
    unnamed x22, local copies, waits for them, and re-layouts  4.99 us
    ppermute x3, starting transfers between devices, shards(): lax.ppermute(pieces[turn], 'people', [(host, source_of(host, turn)) for h...  3.24 us
  transfers between devices with their start and end apart: 15, of which 7 were waited for; matrix products, arithmetic and copies ran while one was open for 0% of the time, Pallas kernels for 6%

profile of v1, /device:TPU:0, one launch (start us, length us, event | category | flops | bytes accessed | tf_op | source)
XLA Modules:
  0.0 98.4 jit_solution(17084635698786685107)
XLA Ops:
  0.0 2.3 %pack.1.refs_0_ = bf16[1088,256]{1,0:T(8,128)(2,1)} custom-call(s32[256,1024]{1,0:T(8,128)} %dosage_ref.1, s32[1,256]{1,0:T(1,128)} %bitcast.4, bf16[48,256]{1,0:T(8,128)(2,1)} %bitcast.3), custom_call_target="tpu_custom_call" | custom-call | tf_op jit(solution)/shard_map/pack/pallas_call | solution.py:505
  2.3 5.0 %collective-permute-start.1 = (bf16[1088,256]{1,0:T(8,128)(2,1)}, bf16[1088,256]{1,0:T(8,128)(2,1)S(1)}, u32[]{:S(2)}, u32[]{:S(2)}) collective-permute-start(bf16[1088,256]{1,0:T(8,128)(2,1)} %pack.1.refs_0_), channel_id=1, source_target_pairs={{0,4},{12,8},{1,5},{13,9},{2,6},{14,10},{3,7},{15,11},{16,20},{28,... | collective-permute-start | bytes 1671176 | tf_op jit(solution)/shard_map/ppermute | solution.py:524
  7.3 0.7 collective-permute-start.3
  8.0 4.0 %collective-permute-start.5 = (bf16[1088,256]{1,0:T(8,128)(2,1)}, bf16[1088,256]{1,0:T(8,128)(2,1)S(1)}, u32[]{:S(2)}, u32[]{:S(2)}) collective-permute-start(bf16[1088,256]{1,0:T(8,128)(2,1)} %pack.1.refs_0_), channel_id=1, source_target_pairs={{12,4},{0,8},{13,5},{1,9},{14,6},{2,10},{15,7},{3,11},{28,20},{16,... | collective-permute-start | bytes 1671176 | tf_op jit(solution)/shard_map/ppermute | solution.py:524
  12.0 8.5 %collective-permute-done.1.refs_2_.refs_6_ = bf16[1088,256]{1,0:T(8,128)(2,1)S(1)} collective-permute-done((bf16[1088,256]{1,0:T(8,128)(2,1)}, bf16[1088,256]{1,0:T(8,128)(2,1)S(1)}, u32[]{:S(2)}, u32[]{:S(2)}) %collective-permute-start.1) | collective-permute-done | bytes 557088 | tf_op jit(solution)/shard_map/ppermute | solution.py:524
  20.6 0.5 collective-permute-start.4
  21.1 10.3 %collective-permute-done.5.refs_4_ = bf16[1088,256]{1,0:T(8,128)(2,1)S(1)} collective-permute-done((bf16[1088,256]{1,0:T(8,128)(2,1)}, bf16[1088,256]{1,0:T(8,128)(2,1)S(1)}, u32[]{:S(2)}, u32[]{:S(2)}) %collective-permute-start.5) | collective-permute-done | bytes 557088 | tf_op jit(solution)/shard_map/ppermute | solution.py:524
  31.4 0.8 copy-done.3
  32.3 0.8 copy-done.4
  33.1 6.1 %early.1 = (f32[1072,1024]{1,0:T(8,128)}, bf16[16,512]{1,0:T(8,128)(2,1)}) custom-call(bf16[1088,256]{1,0:T(8,128)(2,1)} %pack.1.refs_0_, bf16[1088,256]{1,0:T(8,128)(2,1)} %copy-done.3, bf16[1088,256]{1,0:T(8,128)(2,1)} %copy-done, bf16[1088,256]{1,0:T(8,128)(2,1)} %copy-done.4), custom_call_target="tpu_custom_call" | custom-call | flops 2248146944 | bytes 8781824 | tf_op jit(solution)/shard_map/early/pallas_call | solution.py:535
  39.3 0.8 copy-done.5
  40.1 22.4 %fit.1 = (bf16[64,2048]{1,0:T(8,128)(2,1)}, bf16[64,2048]{1,0:T(8,128)(2,1)}) custom-call(f32[5]{0:T(128)} %ridges_ref.3, f32[1072,1024]{1,0:T(8,128)} %get-tuple-element.14.early_ref, bf16[1088,256]{1,0:T(8,128)(2,1)} %pack.1.refs_0_, bf16[1088,256]{1,0:T(8,128)(2,1)} %copy-done.3, bf16[1088,256]{1,0:T(8,128)(2,1)} %copy-done.1, ...), custom_call_target="tpu_custom_call" | custom-call | tf_op jit(solution)/shard_map/fit/pallas_call | solution.py:555
  62.5 0.5 collective-permute-start.7
  63.0 1.4 %collective-permute-done.7.received_ref = bf16[64,2048]{1,0:T(8,128)(2,1)S(1)} collective-permute-done((bf16[64,2048]{1,0:T(8,128)(2,1)}, bf16[64,2048]{1,0:T(8,128)(2,1)S(1)}, u32[]{:S(2)}, u32[]{:S(2)}) %collective-permute-start.7) | collective-permute-done | bytes 262176 | tf_op jit(solution)/shard_map/ppermute | solution.py:515
  64.4 0.7 copy-done.7
  65.1 1.7 %join.1 = (bf16[64,512]{1,0:T(8,128)(2,1)}, bf16[64,512]{1,0:T(8,128)(2,1)}, bf16[64,512]{1,0:T(8,128)(2,1)}, bf16[64,512]{1,0:T(8,128)(2,1)}) custom-call(bf16[64,2048]{1,0:T(8,128)(2,1)} %get-tuple-element.15.keep_ref, bf16[64,2048]{1,0:T(8,128)(2,1)} %copy-done.7), custom_call_target="tpu_custom_call" | custom-call | tf_op jit(solution)/shard_map/join/pallas_call | solution.py:580
  66.9 1.3 %collective-permute-start.8 = (bf16[64,512]{1,0:T(8,128)(2,1)}, bf16[64,512]{1,0:T(8,128)(2,1)S(1)}, u32[]{:S(2)}, u32[]{:S(2)}) collective-permute-start(bf16[64,512]{1,0:T(8,128)(2,1)} %get-tuple-element.17), channel_id=1, source_target_pairs={{4,0},{8,12},{5,1},{9,13},{6,2},{10,14},{7,3},{11,15},{20,16},{24,... | collective-permute-start | bytes 196616 | tf_op jit(solution)/shard_map/ppermute | solution.py:589
  68.1 1.3 %collective-permute-start.9 = (bf16[64,512]{1,0:T(8,128)(2,1)}, bf16[64,512]{1,0:T(8,128)(2,1)S(1)}, u32[]{:S(2)}, u32[]{:S(2)}) collective-permute-start(bf16[64,512]{1,0:T(8,128)(2,1)} %get-tuple-element.18), channel_id=1, source_target_pairs={{4,12},{8,0},{5,13},{9,1},{6,14},{10,2},{7,15},{11,3},{20,28},{24,... | collective-permute-start | bytes 196616 | tf_op jit(solution)/shard_map/ppermute | solution.py:589
  69.4 0.7 collective-permute-start.10
  70.2 4.6 %collective-permute-done.8 = bf16[64,512]{1,0:T(8,128)(2,1)S(1)} collective-permute-done((bf16[64,512]{1,0:T(8,128)(2,1)}, bf16[64,512]{1,0:T(8,128)(2,1)S(1)}, u32[]{:S(2)}, u32[]{:S(2)}) %collective-permute-start.8) | collective-permute-done | bytes 65568 | tf_op jit(solution)/shard_map/ppermute | solution.py:589
  74.7 2.3 %collective-permute-done.9 = bf16[64,512]{1,0:T(8,128)(2,1)S(1)} collective-permute-done((bf16[64,512]{1,0:T(8,128)(2,1)}, bf16[64,512]{1,0:T(8,128)(2,1)S(1)}, u32[]{:S(2)}, u32[]{:S(2)}) %collective-permute-start.9) | collective-permute-done | bytes 65568 | tf_op jit(solution)/shard_map/ppermute | solution.py:589
  77.1 1.5 %select_select_fusion = (bf16[64,512]{1,0:T(8,128)(2,1)S(1)}, bf16[64,512]{1,0:T(8,128)(2,1)}) fusion(bf16[64,512]{1,0:T(8,128)(2,1)S(1)} %collective-permute-done.8, bf16[64,512]{1,0:T(8,128)(2,1)S(1)} %collective-permute-done.9, bf16[64,512]{1,0:T(8,128)(2,1)S(1)} %collective-permute-done.10, bf16[64,512]{1,0:T(8,128)(2,1)} %get-tuple-element.20, ...), kind=kLoop, calls=%fused_computation | loop fusion | flops 196608 | bytes 393222 | tf_op jit(solution)/shard_map/jit(_where)/select_n | solution.py:603
  78.5 1.5 %collective-permute-start.11 = (bf16[64,512]{1,0:T(8,128)(2,1)S(1)}, bf16[64,512]{1,0:T(8,128)(2,1)S(1)}, u32[]{:S(2)}, u32[]{:S(2)}) collective-permute-start(bf16[64,512]{1,0:T(8,128)(2,1)S(1)} %get-tuple-element.21), channel_id=1, source_target_pairs={{0,2},{2,0},{1,3},{3,1},{4,6},{6,4},{5,7},{7,5},{8,10},{10,8},{9,1... | collective-permute-start | bytes 196616 | tf_op jit(solution)/shard_map/ppermute | solution.py:609
  80.0 2.8 %collective-permute-done.11.refs_1_.refs_5_ = bf16[64,512]{1,0:T(8,128)(2,1)S(1)} collective-permute-done((bf16[64,512]{1,0:T(8,128)(2,1)S(1)}, bf16[64,512]{1,0:T(8,128)(2,1)S(1)}, u32[]{:S(2)}, u32[]{:S(2)}) %collective-permute-start.11) | collective-permute-done | bytes 65568 | tf_op jit(solution)/shard_map/ppermute | solution.py:609
  82.8 0.6 copy-done.6
  83.4 1.9 %moment.1.refs_0_ = f32[16,128]{1,0:T(8,128)} custom-call(bf16[16,512]{1,0:T(8,128)(2,1)} %get-tuple-element.13.pheno_ref, bf16[64,512]{1,0:T(8,128)(2,1)} %get-tuple-element.22.refs_0_.refs_4_, bf16[64,512]{1,0:T(8,128)(2,1)} %copy-done.6), custom_call_target="tpu_custom_call" | custom-call | tf_op jit(solution)/shard_map/moment/pallas_call | solution.py:618
  85.3 3.8 %collective-permute-start.12 = (f32[16,128]{1,0:T(8,128)}, f32[16,128]{1,0:T(8,128)S(1)}, u32[]{:S(2)}, u32[]{:S(2)}) collective-permute-start(f32[16,128]{1,0:T(8,128)} %moment.1.refs_0_), channel_id=1, source_target_pairs={{0,8},{4,12},{8,0},{12,4},{1,9},{5,13},{9,1},{13,5},{2,10},{6,14},... | collective-permute-start | bytes 24584 | tf_op jit(solution)/shard_map/ppermute | solution.py:628
  89.1 3.8 %collective-permute-start.14 = (f32[16,128]{1,0:T(8,128)}, f32[16,128]{1,0:T(8,128)S(1)}, u32[]{:S(2)}, u32[]{:S(2)}) collective-permute-start(f32[16,128]{1,0:T(8,128)} %moment.1.refs_0_), channel_id=1, source_target_pairs={{0,12},{4,0},{8,4},{12,8},{1,13},{5,1},{9,5},{13,9},{2,14},{6,2},{... | collective-permute-start | bytes 24584 | tf_op jit(solution)/shard_map/ppermute | solution.py:628
  92.9 1.8 %collective-permute-done.13.refs_2_ = f32[16,128]{1,0:T(8,128)S(1)} collective-permute-done((f32[16,128]{1,0:T(8,128)}, f32[16,128]{1,0:T(8,128)S(1)}, u32[]{:S(2)}, u32[]{:S(2)}) %collective-permute-start.13) | collective-permute-done | bytes 8224 | tf_op jit(solution)/shard_map/ppermute | solution.py:628
  94.8 0.6 copy-done.9
  95.3 0.6 copy-done.10
  95.9 2.5 %second.1 = f32[5,12,512]{2,1,0:T(8,128)} custom-call(f32[5]{0:T(128)} %ridges_ref.3, f32[16,128]{1,0:T(8,128)} %moment.1.refs_0_, f32[16,128]{1,0:T(8,128)} %copy-done.8, f32[16,128]{1,0:T(8,128)} %copy-done.9, f32[16,128]{1,0:T(8,128)} %copy-done.10, bf16[64,512]{1,0:T(8,128)(2,1)} %get-tuple-element.22.refs_0_.refs_4_, bf16[64,512]{1,0:T(8,128)(2,1)} %copy-done.6), custom_call_target="tpu_custom_call" | custom-call | tf_op jit(solution)/shard_map/second/pallas_call | solution.py:634
  (27 shorter events, 0.1 us)
Async XLA Ops:
  2.3 18.3 %collective-permute-start.1 = (bf16[1088,256]{1,0:T(8,128)(2,1)}, bf16[1088,256]{1,0:T(8,128)(2,1)S(1)}, u32[]{:S(2)}, u32[]{:S(2)}) collective-permute-start(bf16[1088,256]{1,0:T(8,128)(2,1)} %pack.1.refs_0_), channel_id=1, source_target_pairs={{0,4},{12,8},{1,5},{13,9},{2,6},{14,10},{3,7},{15,11},{16,20},{28,... | collective-permute-start | bytes 1671176 | tf_op jit(solution)/shard_map/ppermute | solution.py:524
  7.3 13.3 %collective-permute-start.3 = (bf16[1088,256]{1,0:T(8,128)(2,1)}, bf16[1088,256]{1,0:T(8,128)(2,1)S(1)}, u32[]{:S(2)}, u32[]{:S(2)}) collective-permute-start(bf16[1088,256]{1,0:T(8,128)(2,1)} %pack.1.refs_0_), channel_id=1, source_target_pairs={{8,4},{4,8},{9,5},{5,9},{10,6},{6,10},{11,7},{7,11},{24,20},{20,24... | collective-permute-start | bytes 1671176 | tf_op jit(solution)/shard_map/ppermute | solution.py:524
  8.0 23.4 %collective-permute-start.5 = (bf16[1088,256]{1,0:T(8,128)(2,1)}, bf16[1088,256]{1,0:T(8,128)(2,1)S(1)}, u32[]{:S(2)}, u32[]{:S(2)}) collective-permute-start(bf16[1088,256]{1,0:T(8,128)(2,1)} %pack.1.refs_0_), channel_id=1, source_target_pairs={{12,4},{0,8},{13,5},{1,9},{14,6},{2,10},{15,7},{3,11},{28,20},{16,... | collective-permute-start | bytes 1671176 | tf_op jit(solution)/shard_map/ppermute | solution.py:524
  12.0 19.5 %collective-permute-start = (bf16[1088,256]{1,0:T(8,128)(2,1)}, bf16[1088,256]{1,0:T(8,128)(2,1)S(1)}, u32[]{:S(2)}, u32[]{:S(2)}) collective-permute-start(bf16[1088,256]{1,0:T(8,128)(2,1)} %pack.1.refs_0_), channel_id=1, source_target_pairs={{0,1},{1,0},{2,3},{3,2},{4,5},{5,4},{6,7},{7,6},{8,9},{9,8},{10,11... | collective-permute-start | bytes 1671176 | tf_op jit(solution)/shard_map/ppermute | solution.py:515
  20.6 10.9 %copy-start = (bf16[1088,256]{1,0:T(8,128)(2,1)}, bf16[1088,256]{1,0:T(8,128)(2,1)S(1)}, u32[]{:S(2)}) copy-start(bf16[1088,256]{1,0:T(8,128)(2,1)S(1)} %collective-permute-done.1.refs_2_.refs_6_) | copy-start | bytes 1671172
  20.6 10.9 %collective-permute-start.2 = (bf16[1088,256]{1,0:T(8,128)(2,1)S(1)}, bf16[1088,256]{1,0:T(8,128)(2,1)S(1)}, u32[]{:S(2)}, u32[]{:S(2)}) collective-permute-start(bf16[1088,256]{1,0:T(8,128)(2,1)S(1)} %collective-permute-done.1.refs_2_.refs_6_), channel_id=1, source_target_pairs={{0,1},{1,0},{2,3},{3,2},{4,5},{5,4},{6,7},{7,6},{8,9},{9,8},{10,11... | collective-permute-start | bytes 1671176 | tf_op jit(solution)/shard_map/ppermute | solution.py:515
  20.6 18.7 %copy-start.1 = (bf16[1088,256]{1,0:T(8,128)(2,1)}, bf16[1088,256]{1,0:T(8,128)(2,1)S(1)}, u32[]{:S(2)}) copy-start(bf16[1088,256]{1,0:T(8,128)(2,1)S(1)} %collective-permute-done.3.refs_2_) | copy-start | bytes 1671172
  20.6 18.7 %collective-permute-start.4 = (bf16[1088,256]{1,0:T(8,128)(2,1)S(1)}, bf16[1088,256]{1,0:T(8,128)(2,1)S(1)}, u32[]{:S(2)}, u32[]{:S(2)}) collective-permute-start(bf16[1088,256]{1,0:T(8,128)(2,1)S(1)} %collective-permute-done.3.refs_2_), channel_id=1, source_target_pairs={{0,1},{1,0},{2,3},{3,2},{4,5},{5,4},{6,7},{7,6},{8,9},{9,8},{10,11... | collective-permute-start | bytes 1671176 | tf_op jit(solution)/shard_map/ppermute | solution.py:515
  31.4 7.9 %copy-start.2 = (bf16[1088,256]{1,0:T(8,128)(2,1)}, bf16[1088,256]{1,0:T(8,128)(2,1)S(1)}, u32[]{:S(2)}) copy-start(bf16[1088,256]{1,0:T(8,128)(2,1)S(1)} %collective-permute-done.5.refs_4_) | copy-start | bytes 1671172
  31.4 7.9 %collective-permute-start.6 = (bf16[1088,256]{1,0:T(8,128)(2,1)S(1)}, bf16[1088,256]{1,0:T(8,128)(2,1)}, u32[]{:S(2)}, u32[]{:S(2)}) collective-permute-start(bf16[1088,256]{1,0:T(8,128)(2,1)S(1)} %collective-permute-done.5.refs_4_), channel_id=1, source_target_pairs={{0,1},{1,0},{2,3},{3,2},{4,5},{5,4},{6,7},{7,6},{8,9},{9,8},{10,11... | collective-permute-start | bytes 1671176 | tf_op jit(solution)/shard_map/ppermute | solution.py:515
  31.4 0.9 copy-start.3
  32.3 0.8 copy-start.4
  39.3 0.9 copy-start.5
  62.5 1.9 %collective-permute-start.7 = (bf16[64,2048]{1,0:T(8,128)(2,1)}, bf16[64,2048]{1,0:T(8,128)(2,1)S(1)}, u32[]{:S(2)}, u32[]{:S(2)}) collective-permute-start(bf16[64,2048]{1,0:T(8,128)(2,1)} %get-tuple-element.16), channel_id=1, source_target_pairs={{0,1},{1,0},{2,3},{3,2},{4,5},{5,4},{6,7},{7,6},{8,9},{9,8},{10,11... | collective-permute-start | bytes 786440 | tf_op jit(solution)/shard_map/ppermute | solution.py:515
  64.4 0.7 copy-start.7
  66.9 7.9 %collective-permute-start.8 = (bf16[64,512]{1,0:T(8,128)(2,1)}, bf16[64,512]{1,0:T(8,128)(2,1)S(1)}, u32[]{:S(2)}, u32[]{:S(2)}) collective-permute-start(bf16[64,512]{1,0:T(8,128)(2,1)} %get-tuple-element.17), channel_id=1, source_target_pairs={{4,0},{8,12},{5,1},{9,13},{6,2},{10,14},{7,3},{11,15},{20,16},{24,... | collective-permute-start | bytes 196616 | tf_op jit(solution)/shard_map/ppermute | solution.py:589
  68.1 8.9 %collective-permute-start.9 = (bf16[64,512]{1,0:T(8,128)(2,1)}, bf16[64,512]{1,0:T(8,128)(2,1)S(1)}, u32[]{:S(2)}, u32[]{:S(2)}) collective-permute-start(bf16[64,512]{1,0:T(8,128)(2,1)} %get-tuple-element.18), channel_id=1, source_target_pairs={{4,12},{8,0},{5,13},{9,1},{6,14},{10,2},{7,15},{11,3},{20,28},{24,... | collective-permute-start | bytes 196616 | tf_op jit(solution)/shard_map/ppermute | solution.py:589
  69.4 7.6 %collective-permute-start.10 = (bf16[64,512]{1,0:T(8,128)(2,1)}, bf16[64,512]{1,0:T(8,128)(2,1)S(1)}, u32[]{:S(2)}, u32[]{:S(2)}) collective-permute-start(bf16[64,512]{1,0:T(8,128)(2,1)} %get-tuple-element.19), channel_id=1, source_target_pairs={{4,8},{8,4},{5,9},{9,5},{6,10},{10,6},{7,11},{11,7},{20,24},{24,20... | collective-permute-start | bytes 196616 | tf_op jit(solution)/shard_map/ppermute | solution.py:589
  78.5 4.3 %collective-permute-start.11 = (bf16[64,512]{1,0:T(8,128)(2,1)S(1)}, bf16[64,512]{1,0:T(8,128)(2,1)S(1)}, u32[]{:S(2)}, u32[]{:S(2)}) collective-permute-start(bf16[64,512]{1,0:T(8,128)(2,1)S(1)} %get-tuple-element.21), channel_id=1, source_target_pairs={{0,2},{2,0},{1,3},{3,1},{4,6},{6,4},{5,7},{7,5},{8,10},{10,8},{9,1... | collective-permute-start | bytes 196616 | tf_op jit(solution)/shard_map/ppermute | solution.py:609
  82.8 0.6 copy-start.6
  85.3 7.6 %collective-permute-start.12 = (f32[16,128]{1,0:T(8,128)}, f32[16,128]{1,0:T(8,128)S(1)}, u32[]{:S(2)}, u32[]{:S(2)}) collective-permute-start(f32[16,128]{1,0:T(8,128)} %moment.1.refs_0_), channel_id=1, source_target_pairs={{0,8},{4,12},{8,0},{12,4},{1,9},{5,13},{9,1},{13,5},{2,10},{6,14},... | collective-permute-start | bytes 24584 | tf_op jit(solution)/shard_map/ppermute | solution.py:628
  89.1 5.7 %collective-permute-start.13 = (f32[16,128]{1,0:T(8,128)}, f32[16,128]{1,0:T(8,128)S(1)}, u32[]{:S(2)}, u32[]{:S(2)}) collective-permute-start(f32[16,128]{1,0:T(8,128)} %moment.1.refs_0_), channel_id=1, source_target_pairs={{0,4},{4,8},{8,12},{12,0},{1,5},{5,9},{9,13},{13,1},{2,6},{6,10},{... | collective-permute-start | bytes 24584 | tf_op jit(solution)/shard_map/ppermute | solution.py:628
  89.1 5.7 %collective-permute-start.14 = (f32[16,128]{1,0:T(8,128)}, f32[16,128]{1,0:T(8,128)S(1)}, u32[]{:S(2)}, u32[]{:S(2)}) collective-permute-start(f32[16,128]{1,0:T(8,128)} %moment.1.refs_0_), channel_id=1, source_target_pairs={{0,12},{4,0},{8,4},{12,8},{1,13},{5,1},{9,5},{13,9},{2,14},{6,2},{... | collective-permute-start | bytes 24584 | tf_op jit(solution)/shard_map/ppermute | solution.py:628
  92.9 1.8 %copy-start.8 = (f32[16,128]{1,0:T(8,128)}, f32[16,128]{1,0:T(8,128)S(1)}, u32[]{:S(2)}) copy-start(f32[16,128]{1,0:T(8,128)S(1)} %collective-permute-done.12.refs_1_) | copy-start | bytes 24580
  94.7 0.6 copy-start.9
  95.3 0.6 copy-start.10
